TPU v7x, 32 devices: a whole 2x2x4 slice. The times are simulated.
32 devices in a mesh: fsdp: 4 (over y, x), ctx: 4 (over z), tp: 2 (over core).
Axes of the slice: x: 2, y: 2, z: 4, core: 2. Of those that a mesh axis runs over, the one named last changes fastest.
Arguments:
- inputs: bfloat16 [4, 1024, 2048], P('fsdp', 'ctx'), may hold values from -6 to 6
- positions: int32 [4, 1024], P('fsdp', 'ctx'), may hold values from 0 to 1535, as said below
- blocks: int32 [4, 1024], P('fsdp', 'ctx'), may hold values from 0 to 7, never falling along the last dimension, each value on 1 to 256 neighbouring positions
- cotangent: bfloat16 [4, 1024, 2048], P('fsdp', 'ctx'), may hold values from -6 to 6
- attn_gain: bfloat16 [2048], P('fsdp'), may hold values from 0.099609375 to 1.8984375
- w_query: bfloat16 [2048, 2048], P('fsdp', 'tp'), may hold values from -0.125 to 0.125
- w_key: bfloat16 [2048, 256], P('fsdp', 'tp'), may hold values from -0.125 to 0.125
- w_value: bfloat16 [2048, 256], P('fsdp', 'tp'), may hold values from -0.125 to 0.125
- w_out: bfloat16 [2048, 2048], P('tp', 'fsdp'), may hold values from -1 to 1
- mlp_gain: bfloat16 [2048], P('fsdp'), may hold values from 0.099609375 to 1.8984375
- w_gate: bfloat16 [2048, 5632], P('fsdp', 'tp'), may hold values from -0.125 to 0.125
- w_up: bfloat16 [2048, 5632], P('fsdp', 'tp'), may hold values from -0.125 to 0.125
- w_down: bfloat16 [5632, 2048], P('tp', 'fsdp'), may hold values from -0.078125 to 0.078125
Outputs:
- output: bfloat16 [4, 1024, 2048], P('fsdp', 'ctx')
- input_grad: float32 [4, 1024, 2048], P('fsdp', 'ctx')
- attn_gain_grad: float32 [2048], P('fsdp')
- query_grad: float32 [2048, 2048], P('fsdp', 'tp')
- key_grad: float32 [2048, 256], P('fsdp', 'tp')
- value_grad: float32 [2048, 256], P('fsdp', 'tp')
- out_grad: float32 [2048, 2048], P('tp', 'fsdp')
- mlp_gain_grad: float32 [2048], P('fsdp')
- gate_grad: float32 [2048, 5632], P('fsdp', 'tp')
- up_grad: float32 [2048, 5632], P('fsdp', 'tp')
- down_grad: float32 [5632, 2048], P('tp', 'fsdp')
Inputs may be any that keep to these rules, and one draw needn't show every extreme that they name: `positions`: positions start at 0 and rise by 1 or 2 from each token to the next along a sequence; in every sequence exactly 512 of these steps are 2. `blocks`: block ids never fall along a sequence; every block holds 1 to 256 tokens.
All inputs are finite; a program needn't handle non-finite values.
Results may differ from a plain program's by a relative error of at most 0.023.
Values may be sent and summed in bfloat16 or wider, within the bound.
A program may use at most 320 MiB of HBM per device.

v0:
```python
import math
import jax
import jax.numpy as jnp
from jax import lax
from jax.sharding import PartitionSpec as P

HD = 64
EPSILON = 1e-05
NEGATIVE = -1e30


def angles(positions, head_size):
    half_size = head_size // 2
    frequency = jnp.exp(
        jnp.arange(half_size, dtype=jnp.float32) * (-2.0 * math.log(10000.0) / head_size)
    )
    turned = positions.astype(jnp.float32)[:, None] * frequency[None, :]
    return (jnp.cos(turned)[:, None, :], jnp.sin(turned)[:, None, :])


def rotate(values, cosine, sine_turn):
    half_size = values.shape[-1] // 2
    first_half = values[..., :half_size]
    second_half = values[..., half_size:]
    return jnp.concatenate(
        [
            first_half * cosine - second_half * sine_turn,
            second_half * cosine + first_half * sine_turn,
        ],
        axis=-1,
    )


def masked_scores(query_four, key_block, key_ids, query_ids, factor):
    scores = (
        jnp.einsum("tkgd,skd->kgts", query_four, key_block, preferred_element_type=jnp.float32)
        * factor
    )
    allowed = key_ids[None, :] <= query_ids[:, None]
    return (jnp.where(allowed, scores, NEGATIVE), allowed)


def norm_back(upstream, normed, scale, gain):
    weighted = upstream * gain
    return scale * (weighted - normed * jnp.mean(weighted * normed, axis=-1, keepdims=True))


def local(
    inputs,
    positions,
    blocks,
    cotangent,
    attn_gain,
    w_query,
    w_key,
    w_value,
    w_out,
    mlp_gain,
    w_gate,
    w_up,
    w_down,
):
    token_rows = inputs[0].astype(jnp.float32)
    place_row = positions[0]
    own_ids = blocks[0]
    back_low = cotangent[0]
    back_full = back_low.astype(jnp.float32)
    tokens = token_rows.shape[0]
    gain_one, query_w, key_w, value_w, gain_two, gate_w, up_w = (
        lax.all_gather(attn_gain, "fsdp", axis=0, tiled=True),
        lax.all_gather(w_query, "fsdp", axis=0, tiled=True),
        lax.all_gather(w_key, "fsdp", axis=0, tiled=True),
        lax.all_gather(w_value, "fsdp", axis=0, tiled=True),
        lax.all_gather(mlp_gain, "fsdp", axis=0, tiled=True),
        lax.all_gather(w_gate, "fsdp", axis=0, tiled=True),
        lax.all_gather(w_up, "fsdp", axis=0, tiled=True),
    )
    out_w, down_w = (
        lax.all_gather(w_out, "fsdp", axis=1, tiled=True),
        lax.all_gather(w_down, "fsdp", axis=1, tiled=True),
    )
    gain_one = gain_one.astype(jnp.float32)
    gain_two = gain_two.astype(jnp.float32)
    scale_one = lax.rsqrt(jnp.mean(token_rows * token_rows, axis=-1, keepdims=True) + EPSILON)
    normed_one = token_rows * scale_one
    input_one = (normed_one * gain_one).astype(jnp.bfloat16)
    query_pre = jnp.dot(input_one, query_w, preferred_element_type=jnp.float32)
    key_pre = jnp.dot(input_one, key_w, preferred_element_type=jnp.float32)
    value_low = jnp.dot(input_one, value_w, preferred_element_type=jnp.float32).astype(jnp.bfloat16)
    cosine, sine_turn = angles(place_row, HD)
    query_rot = rotate(query_pre.reshape(tokens, -1, HD), cosine, sine_turn).astype(jnp.bfloat16)
    key_rot = rotate(key_pre.reshape(tokens, -1, HD), cosine, sine_turn).astype(jnp.bfloat16)
    kv_heads = key_rot.shape[1]
    grouping = query_rot.shape[1] // kv_heads
    query_four = query_rot.reshape(tokens, kv_heads, grouping, HD)
    all_keys, all_values, all_ids = (
        lax.all_gather(key_rot.reshape(tokens, kv_heads * HD), "ctx", axis=0, tiled=True),
        lax.all_gather(value_low, "ctx", axis=0, tiled=True),
        lax.all_gather(own_ids, "ctx", axis=0, tiled=True),
    )
    length = all_keys.shape[0]
    block_rows = math.gcd(length, 512)
    block_total = length // block_rows
    key_blocks = all_keys.reshape(block_total, block_rows, kv_heads, HD)
    value_blocks = all_values.reshape(block_total, block_rows, kv_heads, HD)
    id_blocks = all_ids.reshape(block_total, block_rows)
    factor = 1.0 / math.sqrt(HD)

    def stats_step(carry_pair, block_item):
        running_top, running_sum = carry_pair
        key_block, key_ids = block_item
        scores, allowed = masked_scores(query_four, key_block, key_ids, own_ids, factor)
        new_top = jnp.maximum(running_top, jnp.max(scores, axis=-1))
        fresh = jnp.where(allowed, jnp.exp(scores - new_top[..., None]), 0.0)
        new_sum = running_sum * jnp.exp(running_top - new_top) + jnp.sum(fresh, axis=-1)
        return ((new_top, new_sum), None)

    start_top = jnp.full((kv_heads, grouping, tokens), NEGATIVE, jnp.float32)
    (row_top, row_sum), _ = lax.scan(
        stats_step, (start_top, jnp.zeros_like(start_top)), (key_blocks, id_blocks)
    )

    def probabilities(key_block, key_ids):
        scores, allowed = masked_scores(query_four, key_block, key_ids, own_ids, factor)
        return jnp.where(allowed, jnp.exp(scores - row_top[..., None]) / row_sum[..., None], 0.0)

    def value_step(mixed_sum, block_item):
        key_block, value_block, key_ids = block_item
        weights_low = probabilities(key_block, key_ids).astype(jnp.bfloat16)
        return (
            mixed_sum
            + jnp.einsum(
                "kgts,skd->tkgd", weights_low, value_block, preferred_element_type=jnp.float32
            ),
            None,
        )

    attended, _ = lax.scan(
        value_step,
        jnp.zeros((tokens, kv_heads, grouping, HD), jnp.float32),
        (key_blocks, value_blocks, id_blocks),
    )
    attended_low = attended.astype(jnp.bfloat16).reshape(tokens, -1)
    hidden = token_rows + lax.psum(
        jnp.dot(attended_low, out_w, preferred_element_type=jnp.float32).astype(jnp.bfloat16), "tp"
    ).astype(jnp.float32)
    scale_two = lax.rsqrt(jnp.mean(hidden * hidden, axis=-1, keepdims=True) + EPSILON)
    normed_two = hidden * scale_two
    input_two = (normed_two * gain_two).astype(jnp.bfloat16)
    gate = jnp.dot(input_two, gate_w, preferred_element_type=jnp.float32)
    up_proj = jnp.dot(input_two, up_w, preferred_element_type=jnp.float32)
    sigmoid_gate = jax.nn.sigmoid(gate)
    silu_gate = gate * sigmoid_gate
    activation = (silu_gate * up_proj).astype(jnp.bfloat16)
    mlp_sum = lax.psum(
        jnp.dot(activation, down_w, preferred_element_type=jnp.float32).astype(jnp.bfloat16), "tp"
    ).astype(jnp.float32)
    output = (hidden + mlp_sum).astype(jnp.bfloat16)
    act_grad = jnp.einsum("td,fd->tf", back_low, down_w, preferred_element_type=jnp.float32)
    down_grad_t = jnp.einsum("td,tf->df", back_low, activation, preferred_element_type=jnp.float32)
    gate_back = (act_grad * up_proj * sigmoid_gate * (1.0 + gate * (1.0 - sigmoid_gate))).astype(
        jnp.bfloat16
    )
    up_back = (act_grad * silu_gate).astype(jnp.bfloat16)
    gate_grad = jnp.einsum("td,tf->df", input_two, gate_back, preferred_element_type=jnp.float32)
    up_grad = jnp.einsum("td,tf->df", input_two, up_back, preferred_element_type=jnp.float32)
    two_partial = jnp.einsum(
        "tf,df->td", gate_back, gate_w, preferred_element_type=jnp.float32
    ) + jnp.einsum("tf,df->td", up_back, up_w, preferred_element_type=jnp.float32)
    input_two_grad = lax.psum(two_partial.astype(jnp.bfloat16), "tp").astype(jnp.float32)
    gain_two_grad = jnp.sum(input_two_grad * normed_two, axis=0)
    hidden_grad = back_full + norm_back(input_two_grad, normed_two, scale_two, gain_two)
    hidden_low = hidden_grad.astype(jnp.bfloat16)
    out_grad_t = jnp.einsum(
        "td,tc->dc", hidden_low, attended_low, preferred_element_type=jnp.float32
    )
    attended_grad = (
        jnp.einsum("td,cd->tc", hidden_low, out_w, preferred_element_type=jnp.float32)
        .astype(jnp.bfloat16)
        .reshape(tokens, kv_heads, grouping, HD)
    )
    row_delta = jnp.einsum("tkgd,tkgd->kgt", attended_grad.astype(jnp.float32), attended)

    def back_step(query_sum, block_item):
        key_block, value_block, key_ids = block_item
        weights_full = probabilities(key_block, key_ids)
        weight_grad = jnp.einsum(
            "tkgd,skd->kgts", attended_grad, value_block, preferred_element_type=jnp.float32
        )
        score_grad = (weights_full * (weight_grad - row_delta[..., None])).astype(jnp.bfloat16)
        value_part = jnp.einsum(
            "kgts,tkgd->skd",
            weights_full.astype(jnp.bfloat16),
            attended_grad,
            preferred_element_type=jnp.float32,
        )
        key_part = (
            jnp.einsum("kgts,tkgd->skd", score_grad, query_four, preferred_element_type=jnp.float32)
            * factor
        )
        query_sum = (
            query_sum
            + jnp.einsum(
                "kgts,skd->tkgd", score_grad, key_block, preferred_element_type=jnp.float32
            )
            * factor
        )
        return (query_sum, (key_part, value_part))

    query_grad_rot, (key_parts, value_parts) = lax.scan(
        back_step,
        jnp.zeros((tokens, kv_heads, grouping, HD), jnp.float32),
        (key_blocks, value_blocks, id_blocks),
    )
    key_total, value_total = (
        lax.psum_scatter(
            key_parts.reshape(length, kv_heads * HD).astype(jnp.bfloat16),
            "ctx",
            scatter_dimension=0,
            tiled=True,
        ).astype(jnp.float32),
        lax.psum_scatter(
            value_parts.reshape(length, kv_heads * HD).astype(jnp.bfloat16),
            "ctx",
            scatter_dimension=0,
            tiled=True,
        ).astype(jnp.float32),
    )
    query_back = (
        rotate(query_grad_rot.reshape(tokens, kv_heads * grouping, HD), cosine, -sine_turn)
        .reshape(tokens, -1)
        .astype(jnp.bfloat16)
    )
    key_back = (
        rotate(key_total.reshape(tokens, kv_heads, HD), cosine, -sine_turn)
        .reshape(tokens, -1)
        .astype(jnp.bfloat16)
    )
    value_back = value_total.astype(jnp.bfloat16)
    query_grad = jnp.einsum("td,tc->dc", input_one, query_back, preferred_element_type=jnp.float32)
    key_grad = jnp.einsum("td,tc->dc", input_one, key_back, preferred_element_type=jnp.float32)
    value_grad = jnp.einsum("td,tc->dc", input_one, value_back, preferred_element_type=jnp.float32)
    one_partial = jnp.einsum("tc,dc->td", query_back, query_w, preferred_element_type=jnp.float32)
    one_partial = one_partial + jnp.einsum(
        "tc,dc->td", key_back, key_w, preferred_element_type=jnp.float32
    )
    one_partial = one_partial + jnp.einsum(
        "tc,dc->td", value_back, value_w, preferred_element_type=jnp.float32
    )
    input_one_grad = lax.psum(one_partial.astype(jnp.bfloat16), "tp").astype(jnp.float32)
    gain_one_grad = jnp.sum(input_one_grad * normed_one, axis=0)
    input_grad = hidden_grad + norm_back(input_one_grad, normed_one, scale_one, gain_one)
    shares = (
        lax.psum_scatter(
            gain_one_grad.astype(jnp.bfloat16), "fsdp", scatter_dimension=0, tiled=True
        ).astype(jnp.float32),
        lax.psum_scatter(
            query_grad.astype(jnp.bfloat16), "fsdp", scatter_dimension=0, tiled=True
        ).astype(jnp.float32),
        lax.psum_scatter(
            key_grad.astype(jnp.bfloat16), "fsdp", scatter_dimension=0, tiled=True
        ).astype(jnp.float32),
        lax.psum_scatter(
            value_grad.astype(jnp.bfloat16), "fsdp", scatter_dimension=0, tiled=True
        ).astype(jnp.float32),
        lax.psum_scatter(
            out_grad_t.astype(jnp.bfloat16), "fsdp", scatter_dimension=0, tiled=True
        ).astype(jnp.float32),
        lax.psum_scatter(
            gain_two_grad.astype(jnp.bfloat16), "fsdp", scatter_dimension=0, tiled=True
        ).astype(jnp.float32),
        lax.psum_scatter(
            gate_grad.astype(jnp.bfloat16), "fsdp", scatter_dimension=0, tiled=True
        ).astype(jnp.float32),
        lax.psum_scatter(
            up_grad.astype(jnp.bfloat16), "fsdp", scatter_dimension=0, tiled=True
        ).astype(jnp.float32),
        lax.psum_scatter(
            down_grad_t.astype(jnp.bfloat16), "fsdp", scatter_dimension=0, tiled=True
        ).astype(jnp.float32),
    )
    shares = (
        lax.psum(shares[0].astype(jnp.bfloat16), "ctx").astype(jnp.float32),
        lax.psum(shares[1].astype(jnp.bfloat16), "ctx").astype(jnp.float32),
        lax.psum(shares[2].astype(jnp.bfloat16), "ctx").astype(jnp.float32),
        lax.psum(shares[3].astype(jnp.bfloat16), "ctx").astype(jnp.float32),
        lax.psum(shares[4].astype(jnp.bfloat16), "ctx").astype(jnp.float32),
        lax.psum(shares[5].astype(jnp.bfloat16), "ctx").astype(jnp.float32),
        lax.psum(shares[6].astype(jnp.bfloat16), "ctx").astype(jnp.float32),
        lax.psum(shares[7].astype(jnp.bfloat16), "ctx").astype(jnp.float32),
        lax.psum(shares[8].astype(jnp.bfloat16), "ctx").astype(jnp.float32),
    )
    return (
        output[None],
        input_grad[None],
        shares[0],
        shares[1],
        shares[2],
        shares[3],
        shares[4].T,
        shares[5],
        shares[6],
        shares[7],
        shares[8].T,
    )


def solution(mesh):
    return jax.shard_map(
        local,
        mesh=mesh,
        in_specs=(
            P("fsdp", "ctx", None),
            P("fsdp", "ctx"),
            P("fsdp", "ctx"),
            P("fsdp", "ctx", None),
            P("fsdp"),
            P("fsdp", "tp"),
            P("fsdp", "tp"),
            P("fsdp", "tp"),
            P("tp", "fsdp"),
            P("fsdp"),
            P("fsdp", "tp"),
            P("fsdp", "tp"),
            P("tp", "fsdp"),
        ),
        out_specs=(
            P("fsdp", "ctx", None),
            P("fsdp", "ctx", None),
            P("fsdp"),
            P("fsdp", "tp"),
            P("fsdp", "tp"),
            P("fsdp", "tp"),
            P("tp", "fsdp"),
            P("fsdp"),
            P("fsdp", "tp"),
            P("fsdp", "tp"),
            P("tp", "fsdp"),
        ),
        check_vma=False,
    )
```

profile of v0, /device:TPU:0, one launch (start us, length us, event | category | flops | bytes accessed | tf_op | source)
XLA Modules:
  0.0 1577.6 jit_solution(1991943502405839874)
XLA Ops:
  8.8 11.5 all_gather.37
  20.3 8.1 all-gather.1
  29.2 14.4 all_gather.38
  44.3 10.7 all-gather
  56.2 13.0 all_gather.40
  70.9 13.8 all_gather.41
  95.1 19.0 %while.39 = (s32[]{:T(128)}, f32[2,8,256]{2,1,0:T(8,128)S(1)}, f32[2,8,256]{2,1,0:T(8,128)S(1)}, s32[2,512]{1,0:T(2,128)S(1)}, s32[1,256]{1,0:T(1,128)S(1)}, /*i...) while((s32[]{:T(128)}, f32[2,8,256]{2,1,0:T(8,128)S(1)}, ...), condition=%wide.region_4.5_spmd.clone, body=%wide.region_1.4_spmd.clone.sunk | while | flops 285364224 | bytes 18046072 | solution.py:119
  114.1 9.6 while.40
  131.6 8.4 all-gather.2
  139.9 8.3 all-reduce.11.cloned.1.call-done
  151.5 113.6 %all-gather.13.cloned.1.call-done = bf16[2048,2816]{1,0:T(8,128)(2,1)} async-done(((bf16[512,2816]{1,0:T(8,128)(2,1)}), bf16[2048,2816]{1,0:T(8,128)(2,1)}) %all-gather.13.cloned.1.call-update) | async-done | bytes 11534352 | tf_op jit(solution)/shard_map/all_gather | solution.py:75
  265.1 9.4 fusion.109
  274.4 106.3 %all-gather.15.cloned.1.call-done = bf16[2048,2816]{1,0:T(8,128)(2,1)} async-done(((bf16[512,2816]{1,0:T(8,128)(2,1)}), bf16[2048,2816]{1,0:T(8,128)(2,1)}) %all-gather.15.cloned.1.call-update) | async-done | bytes 11534352 | tf_op jit(solution)/shard_map/all_gather | solution.py:76
  380.8 9.0 fusion.110
  389.7 106.5 %all-gather.17.cloned.1.call-done = bf16[2816,2048]{1,0:T(8,128)(2,1)} async-done(((bf16[2816,512]{1,0:T(8,128)(2,1)}), bf16[2816,2048]{1,0:T(8,128)(2,1)}) %all-gather.17.cloned.1.call-update) | async-done | bytes 11534352 | tf_op jit(solution)/shard_map/all_gather | solution.py:80
  496.3 11.5 multiply_convert_fusion
  514.8 8.4 fusion.68
  523.4 19.7 %all-reduce.13.cloned.1.call-done = bf16[256,2048]{1,0:T(8,128)(2,1)} async-done(((bf16[256,2048]{1,0:T(8,128)(2,1)}), bf16[256,2048]{1,0:T(8,128)(2,1)}) %all-reduce.13.cloned.1.call-update) | async-done | bytes 1048592 | tf_op jit(solution)/shard_map/psum | solution.py:170
  553.5 35.6 %while.41 = (s32[]{:T(128)}, f32[256,2,8,64]{0,3,2,1:T(8,128)S(1)}, bf16[2,512,2,64]{1,3,2,0:T(8,128)(2,1)}, bf16[2,512,2,64]{1,3,2,0:T(8,128)(2,1)}, bf16[2,512...) while((s32[]{:T(128)}, f32[256,2,8,64]{0,3,2,1:T(8,128)S(1)}, ...), condition=%wide.region_13.14_spmd.clone, body=%wide.region_12.13_spmd.clone.sunk | while | flops 1362034688 | bytes 98753912 | solution.py:210
  593.2 18.9 %reduce-scatter.10.cloned.1.call-done = bf16[256,128]{0,1:T(8,128)(2,1)} async-done(((bf16[1024,128]{0,1:T(8,128)(2,1)}), bf16[256,128]{0,1:T(8,128)(2,1)}) %reduce-scatter.10.cloned.1.call-update) | async-done | bytes 65552 | tf_op jit(solution)/shard_map/reduce_scatter | solution.py:216
  614.5 18.4 %reduce-scatter.12.cloned.1.call-done = bf16[256,128]{0,1:T(8,128)(2,1)} async-done(((bf16[1024,128]{0,1:T(8,128)(2,1)}), bf16[256,128]{0,1:T(8,128)(2,1)}) %reduce-scatter.12.cloned.1.call-update) | async-done | bytes 65552 | tf_op jit(solution)/shard_map/reduce_scatter | solution.py:222
  646.2 7.5 convolution_convert_fusion.1
  671.1 8.7 convolution_convert_fusion.4
  686.6 56.1 %reduce-scatter.20.cloned.1.call-done = bf16[512,1024]{1,0:T(8,128)(2,1)} async-done(((bf16[2048,1024]{1,0:T(8,128)(2,1)}), bf16[512,1024]{1,0:T(8,128)(2,1)}) %reduce-scatter.20.cloned.1.call-update) | async-done | bytes 1048592 | tf_op jit(solution)/shard_map/reduce_scatter | solution.py:266
  742.7 56.5 %reduce-scatter.14.cloned.1.call-done = bf16[512,1024]{1,0:T(8,128)(2,1)} async-done(((bf16[2048,1024]{1,0:T(8,128)(2,1)}), bf16[512,1024]{1,0:T(8,128)(2,1)}) %reduce-scatter.14.cloned.1.call-update) | async-done | bytes 1048592 | tf_op jit(solution)/shard_map/reduce_scatter | solution.py:257
  799.2 115.1 %reduce-scatter.22.cloned.1.call-done = bf16[512,2816]{1,0:T(8,128)(2,1)} async-done(((bf16[2048,2816]{1,0:T(8,128)(2,1)}), bf16[512,2816]{1,0:T(8,128)(2,1)}) %reduce-scatter.22.cloned.1.call-update) | async-done | bytes 2883600 | tf_op jit(solution)/shard_map/reduce_scatter | solution.py:272
  914.3 115.1 %reduce-scatter.24.cloned.1.call-done = bf16[512,2816]{1,0:T(8,128)(2,1)} async-done(((bf16[2048,2816]{1,0:T(8,128)(2,1)}), bf16[512,2816]{1,0:T(8,128)(2,1)}) %reduce-scatter.24.cloned.1.call-update) | async-done | bytes 2883600 | tf_op jit(solution)/shard_map/reduce_scatter | solution.py:275
  1029.4 115.1 %reduce-scatter.26.cloned.1.call-done = bf16[512,2816]{0,1:T(8,128)(2,1)} async-done(((bf16[2048,2816]{0,1:T(8,128)(2,1)}), bf16[512,2816]{0,1:T(8,128)(2,1)}) %reduce-scatter.26.cloned.1.call-update) | async-done | bytes 2883600 | tf_op jit(solution)/shard_map/reduce_scatter | solution.py:278
  1146.4 22.2 %all-reduce.17.cloned.1.call-done = (bf16[256,2048]{1,0:T(8,128)(2,1)}, bf16[256,2048]{1,0:T(8,128)(2,1)}) async-done(((bf16[256,2048]{1,0:T(8,128)(2,1)}, bf16[256,2048]{1,0:T(8,128)(2,1)}), (bf16[256,2048]{1,0:T(8,128)(2,1)}, bf16[256,2048]{1,0:T(8,128)(2,1)})) %all-reduce.17.cloned.1.call-update) | async-done | bytes 2097168 | tf_op jit(solution)/shard_map/psum | solution.py:155
  1170.7 10.3 all-reduce.4
  1181.1 12.3 all-reduce.2
  1200.1 353.1 %all-reduce.15.cloned.1.call-done = (bf16[1024,512]{0,1:T(8,128)(2,1)}, bf16[512,1024]{1,0:T(8,128)(2,1)}, bf16[512,128]{1,0:T(8,128)(2,1)}, bf16[512,128]{1,0:T...) async-done(((bf16[1024,512]{0,1:T(8,128)(2,1)}, bf16[512,1024]{1,0:T(8,128)(2,1)}, bf16[512,128]{1,0:T(8,128)(2,1)}, ...) | async-done | bytes 11010064 | tf_op jit(solution)/shard_map/psum | solution.py:287
  (259 shorter events, 179.3 us)
Async XLA Ops:
  7.2 21.2 %copy-start.2 = (bf16[1,256,2048]{2,1,0:T(8,128)(2,1)S(1)}, bf16[1,256,2048]{2,1,0:T(8,128)(2,1)}, u32[]{:S(2)}) copy-start(bf16[1,256,2048]{2,1,0:T(8,128)(2,1)} %param.19) | copy-start | bytes 3145732
  7.2 77.7 %all-gather.9.cloned.1.call-start = ((), (), s32[]{:S(2)}) async-start(), calls=%async_computation.9 | async-start | bytes 5242880 | tf_op jit(solution)/shard_map/all_gather | solution.py:71
  7.9 117.1 %all-gather.11.cloned.1.call-start = ((), (), s32[]{:S(2)}) async-start(), calls=%async_computation.10 | async-start | bytes 5242880 | tf_op jit(solution)/shard_map/all_gather | solution.py:79
  8.7 139.6 %all-reduce.11.cloned.1.call-start = ((), (), s32[]{:S(2)}) async-start(), calls=%async_computation.11 | async-start | bytes 2097152 | tf_op jit(solution)/shard_map/psum | solution.py:144
  20.3 23.6 %copy-start.19 = (bf16[2048,128]{1,0:T(8,128)(2,1)}, bf16[2048,128]{1,0:T(8,128)(2,1)S(1)}, u32[]{:S(2)}) copy-start(bf16[2048,128]{1,0:T(8,128)(2,1)S(1)} %all_gather.37) | copy-start | bytes 1572868
  28.4 63.0 %copy-start.29 = (f32[4,1,512]{2,1,0:T(1,128)}, f32[4,1,512]{2,1,0:T(1,128)S(1)}, u32[]{:S(2)}) copy-start(f32[4,1,512]{2,1,0:T(1,128)S(1)} %convert_element_type.277) | copy-start | bytes 24580
  28.7 62.7 %copy-start.41 = (f32[256]{0:T(256)}, f32[256]{0:T(256)S(1)}, u32[]{:S(2)}) copy-start(f32[256]{0:T(256)S(1)} %add_rsqrt_fusion.1) | copy-start | bytes 3076
  28.7 27.4 %copy-start.37 = (bf16[512,128]{1,0:T(8,128)(2,1)S(1)}, bf16[512,128]{1,0:T(8,128)(2,1)}, u32[]{:S(2)}) copy-start(bf16[512,128]{1,0:T(8,128)(2,1)} %param.25) | copy-start | bytes 393220
  70.8 24.1 %copy-start.24 = (f32[256,32]{0,1:T(8,128)}, f32[256,32]{0,1:T(8,128)S(1)}, u32[]{:S(2)}) copy-start(f32[256,32]{0,1:T(8,128)S(1)} %get-tuple-element.472) | copy-start | bytes 98308
  129.7 135.4 %all-gather.13.cloned.1.call-start = ((), (), s32[]{:S(2)}) async-start(), calls=%async_computation.12 | async-start | bytes 14417920 | tf_op jit(solution)/shard_map/all_gather | solution.py:75
  130.3 250.5 %all-gather.15.cloned.1.call-start = ((), (), s32[]{:S(2)}) async-start(), calls=%async_computation.13 | async-start | bytes 14417920 | tf_op jit(solution)/shard_map/all_gather | solution.py:76
  130.9 365.4 %all-gather.17.cloned.1.call-start = ((), (), s32[]{:S(2)}) async-start(), calls=%async_computation.14 | async-start | bytes 14417920 | tf_op jit(solution)/shard_map/all_gather | solution.py:80
  131.5 411.6 %all-reduce.13.cloned.1.call-start = ((), (), s32[]{:S(2)}) async-start(), calls=%async_computation.15 | async-start | bytes 2097152 | tf_op jit(solution)/shard_map/psum | solution.py:170
  151.5 229.2 %copy-start.6 = (bf16[256,2048]{1,0:T(8,128)(2,1)S(1)}, bf16[256,2048]{1,0:T(8,128)(2,1)}, u32[]{:S(2)}) copy-start(bf16[256,2048]{1,0:T(8,128)(2,1)} %multiply_convert_fusion.3) | copy-start | bytes 3145732
  523.3 88.8 %reduce-scatter.10.cloned.1.call-start = ((), (), s32[]{:S(2)}) async-start(), calls=%async_computation.16 | async-start | bytes 327680 | tf_op jit(solution)/shard_map/reduce_scatter | solution.py:216
  589.1 23.9 %copy-start.25 = (f32[256,32]{0,1:T(8,128)S(1)}, f32[256,32]{0,1:T(8,128)}, u32[]{:S(2)}) copy-start(f32[256,32]{0,1:T(8,128)} %copy-done.24) | copy-start | bytes 98308
  589.1 23.9 %copy-start.28 = (f32[256,32]{0,1:T(8,128)S(1)}, f32[256,32]{0,1:T(8,128)}, u32[]{:S(2)}) copy-start(f32[256,32]{0,1:T(8,128)} %get-tuple-element.470) | copy-start | bytes 98308
  589.1 23.9 %copy-start.30 = (f32[4,1,512]{2,1,0:T(1,128)S(1)}, f32[4,1,512]{2,1,0:T(1,128)}, u32[]{:S(2)}) copy-start(f32[4,1,512]{2,1,0:T(1,128)} %copy-done.29) | copy-start | bytes 24580
  589.1 24.0 %copy-start.42 = (f32[256]{0:T(256)S(1)}, f32[256]{0:T(256)}, u32[]{:S(2)}) copy-start(f32[256]{0:T(256)} %copy-done.41) | copy-start | bytes 3076
  591.1 41.9 %reduce-scatter.12.cloned.1.call-start = ((), (), s32[]{:S(2)}) async-start(), calls=%async_computation.17 | async-start | bytes 327680 | tf_op jit(solution)/shard_map/reduce_scatter | solution.py:222
  593.1 90.7 %reduce-scatter.16.cloned.1.call-start = ((), (), s32[]{:S(2)}) async-start(), calls=%async_computation.19 | async-start | bytes 655360 | tf_op jit(solution)/shard_map/reduce_scatter | solution.py:260
  614.5 20.8 %copy-start.27 = (bf16[256,2,8,64]{0,3,2,1:T(8,128)(2,1)S(1)}, bf16[256,2,8,64]{0,3,2,1:T(8,128)(2,1)}, u32[]{:S(2)}) copy-start(bf16[256,2,8,64]{0,3,2,1:T(8,128)(2,1)} %copy-done.26) | copy-start | bytes 1572868
  614.5 72.1 %reduce-scatter.18.cloned.1.call-start = ((), (), s32[]{:S(2)}) async-start(), calls=%async_computation.20 | async-start | bytes 655360 | tf_op jit(solution)/shard_map/reduce_scatter | solution.py:263
  635.2 107.5 %reduce-scatter.20.cloned.1.call-start = ((), (), s32[]{:S(2)}) async-start(), calls=%async_computation.21 | async-start | bytes 5242880 | tf_op jit(solution)/shard_map/reduce_scatter | solution.py:266
  641.3 157.9 %reduce-scatter.14.cloned.1.call-start = ((), (), s32[]{:S(2)}) async-start(), calls=%async_computation.18 | async-start | bytes 5242880 | tf_op jit(solution)/shard_map/reduce_scatter | solution.py:257
  645.0 269.3 %reduce-scatter.22.cloned.1.call-start = ((), (), s32[]{:S(2)}) async-start(), calls=%async_computation.22 | async-start | bytes 14417920 | tf_op jit(solution)/shard_map/reduce_scatter | solution.py:272
  653.8 375.6 %reduce-scatter.24.cloned.1.call-start = ((), (), s32[]{:S(2)}) async-start(), calls=%async_computation.23 | async-start | bytes 14417920 | tf_op jit(solution)/shard_map/reduce_scatter | solution.py:275
  661.2 483.4 %reduce-scatter.26.cloned.1.call-start = ((), (), s32[]{:S(2)}) async-start(), calls=%async_computation.24 | async-start | bytes 14417920 | tf_op jit(solution)/shard_map/reduce_scatter | solution.py:278
  669.8 498.8 %all-reduce.17.cloned.1.call-start = ((), (), s32[]{:S(2)}) async-start(), calls=%async_computation.26 | async-start | bytes 4194304 | tf_op jit(solution)/shard_map/psum | solution.py:155
  683.7 869.4 %all-reduce.15.cloned.1.call-start = ((), (), s32[]{:S(2)}) async-start(), calls=%async_computation.25 | async-start | bytes 22020096 | tf_op jit(solution)/shard_map/psum | solution.py:287
  1144.5 26.1 %copy-start.43 = (bf16[2048]{0:T(1024)(128)(2,1)S(1)}, bf16[2048]{0:T(1024)(128)(2,1)}, u32[]{:S(2)}) copy-start(bf16[2048]{0:T(1024)(128)(2,1)} %get-tuple-element.380) | copy-start | bytes 12292
  1144.6 50.0 %copy-start.5 = (bf16[256,2048]{1,0:T(8,128)(2,1)S(1)}, bf16[256,2048]{1,0:T(8,128)(2,1)}, u32[]{:S(2)}) copy-start(bf16[256,2048]{1,0:T(8,128)(2,1)} %all-reduce.11.cloned.1.call-done) | copy-start | bytes 3145732
  (41 other events, 175.1 us)
Sparse Core Ops, SparseCore 0:
  9.9 59.6 all-gather.8
  71.4 52.5 all-gather.10
  129.8 18.3 all-reduce.10
  150.1 114.9 all-gather.12
  266.9 113.7 all-gather.14
  382.6 113.6 all-gather.16
  523.4 19.5 all-reduce.12
  591.2 20.8 reduce-scatter.9
  615.0 17.8 reduce-scatter.11
  635.6 23.0 reduce-scatter.15
  661.8 24.7 reduce-scatter.17
  690.0 52.6 reduce-scatter.19
  746.5 52.6 reduce-scatter.13
  802.2 112.1 reduce-scatter.21
  917.3 112.0 reduce-scatter.23
  1032.4 112.0 reduce-scatter.25
  1147.3 21.2 all-reduce.16
  1172.3 380.7 all-reduce.14
where the time goes:
time: 1590 us; the launch traced here: 1580 us
  waiting for transfers between devices  1230 us (77%)
  matrix products  157 us (10%)
  blocking collectives  102 us (6%)
  other arithmetic  46.7 us (3%)
  local copies, waits for them, and re-layouts  23.8 us (1%)
  between operations  16 us (1%)
    psum x1, waiting for transfers between devices, local(): lax.psum(shares[4].astype(jnp.bfloat16), 'ctx').astype(jnp.float32)  353 us
    reduce_scatter x1, waiting for transfers between devices, local(): lax.psum_scatter(gate_grad.astype(jnp.bfloat16), 'fsdp', scatter_dimensio...  115 us
    reduce_scatter x1, waiting for transfers between devices, local(): lax.psum_scatter(down_grad_t.astype(jnp.bfloat16), 'fsdp', scatter_dimens...  115 us
    reduce_scatter x1, waiting for transfers between devices, local(): lax.psum_scatter(up_grad.astype(jnp.bfloat16), 'fsdp', scatter_dimension=...  115 us
    all_gather x1, waiting for transfers between devices, local(): lax.all_gather(w_gate, 'fsdp', axis=0, tiled=True)  114 us
    all_gather x1, waiting for transfers between devices, local(): lax.all_gather(w_down, 'fsdp', axis=1, tiled=True)  107 us
    all_gather x1, waiting for transfers between devices, local(): lax.all_gather(w_up, 'fsdp', axis=0, tiled=True)  106 us
    reduce_scatter x1, waiting for transfers between devices, local(): lax.psum_scatter(query_grad.astype(jnp.bfloat16), 'fsdp', scatter_dimensi...  56.5 us
  transfers between devices with their start and end apart: 18, of which 15 were waited for; matrix products, arithmetic and copies ran while one was open for 8% of the time, Pallas kernels for 0%

commit v1 on v0

--- a/solution.py
+++ b/solution.py
@@ -60,6 +60,11 @@
     w_up,
     w_down,
 ):
+
+    def define_the_paths(q_in):
+        formed = lax.all_gather(q_in, axis_name="ctx")
+        return jnp.sum(formed, 0)
+
     token_rows = inputs[0].astype(jnp.float32)
     place_row = positions[0]
     own_ids = blocks[0]
@@ -284,7 +289,7 @@
         lax.psum(shares[1].astype(jnp.bfloat16), "ctx").astype(jnp.float32),
         lax.psum(shares[2].astype(jnp.bfloat16), "ctx").astype(jnp.float32),
         lax.psum(shares[3].astype(jnp.bfloat16), "ctx").astype(jnp.float32),
-        lax.psum(shares[4].astype(jnp.bfloat16), "ctx").astype(jnp.float32),
+        define_the_paths(shares[4].astype(jnp.bfloat16)).astype(jnp.float32),
         lax.psum(shares[5].astype(jnp.bfloat16), "ctx").astype(jnp.float32),
         lax.psum(shares[6].astype(jnp.bfloat16), "ctx").astype(jnp.float32),
         lax.psum(shares[7].astype(jnp.bfloat16), "ctx").astype(jnp.float32),

time: 1590 us -> 1640 us (1.031)
  waiting for transfers between devices: 1230 us -> 1270 us
    all_gather x0 -> x1, waiting for transfers between devices: none -> 52.6 us  [define_the_paths(): formed = lax.all_gather(q_in, axis_name='ctx')]
    reduce_scatter x1, waiting for transfers between devices: 56.1 us -> 10.4 us  [local(): lax.psum_scatter(out_grad_t.astype(jnp.bfloat16), 'fsdp', scatter_dimensi...]
    reduce_scatter x1, waiting for transfers between devices: 0.02 us -> 27.8 us  [local(): lax.psum_scatter(key_grad.astype(jnp.bfloat16), 'fsdp', scatter_dimension...]
    reduce_scatter x1, waiting for transfers between devices: 2.77 us -> 27.5 us  [local(): lax.psum_scatter(value_grad.astype(jnp.bfloat16), 'fsdp', scatter_dimensi...]
  transfers between devices with their start and end apart: 18 -> 19, of which waited for: 15 -> 17; matrix products, arithmetic and copies ran while one was open for 8% -> 8% of each run, Pallas kernels for 0% -> 0%
where the time goes in v1:
time: 1640 us; the launch traced here: 1630 us
  waiting for transfers between devices  1270 us (77%)
  matrix products  152 us (9%)
  blocking collectives  104 us (6%)
  other arithmetic  46.9 us (3%)
  local copies, waits for them, and re-layouts  33.8 us (2%)
    psum x1, waiting for transfers between devices, local(): lax.psum(shares[1].astype(jnp.bfloat16), 'ctx').astype(jnp.float32)  342 us
    reduce_scatter x1, waiting for transfers between devices, local(): lax.psum_scatter(gate_grad.astype(jnp.bfloat16), 'fsdp', scatter_dimensio...  115 us
    reduce_scatter x1, waiting for transfers between devices, local(): lax.psum_scatter(down_grad_t.astype(jnp.bfloat16), 'fsdp', scatter_dimens...  115 us
    reduce_scatter x1, waiting for transfers between devices, local(): lax.psum_scatter(up_grad.astype(jnp.bfloat16), 'fsdp', scatter_dimension=...  115 us
    all_gather x1, waiting for transfers between devices, local(): lax.all_gather(w_gate, 'fsdp', axis=0, tiled=True)  115 us
    all_gather x1, waiting for transfers between devices, local(): lax.all_gather(w_up, 'fsdp', axis=0, tiled=True)  107 us
    all_gather x1, waiting for transfers between devices, local(): lax.all_gather(w_down, 'fsdp', axis=1, tiled=True)  107 us
    reduce_scatter x1, waiting for transfers between devices, local(): lax.psum_scatter(query_grad.astype(jnp.bfloat16), 'fsdp', scatter_dimensi...  56.5 us
  transfers between devices with their start and end apart: 19, of which 17 were waited for; matrix products, arithmetic and copies ran while one was open for 8% of the time, Pallas kernels for 0%

profile of v1, /device:TPU:0, one launch (start us, length us, event | category | flops | bytes accessed | tf_op | source)
XLA Modules:
  0.0 1628.4 jit_solution(8851682597219578639)
XLA Ops:
  8.8 9.5 all-gather.2
  18.7 14.8 all_gather.46
  37.0 14.2 all_gather.47
  53.0 10.9 all-gather
  65.1 10.5 all_gather.43
  77.0 13.9 all_gather.44
  101.8 18.7 %while.39 = (s32[]{:T(128)}, f32[2,8,256]{2,1,0:T(8,128)S(1)}, f32[2,8,256]{2,1,0:T(8,128)S(1)}, s32[2,512]{1,0:T(2,128)S(1)}, s32[1,256]{1,0:T(1,128)S(1)}, /*i...) while((s32[]{:T(128)}, f32[2,8,256]{2,1,0:T(8,128)S(1)}, ...), condition=%wide.region_4.5_spmd.clone, body=%wide.region_1.4_spmd.clone.sunk | while | flops 285364224 | bytes 18046064 | solution.py:124
  142.0 8.8 all-reduce.11.cloned.1.call-done
  153.1 114.6 %all-gather.15.cloned.1.call-done = bf16[2048,2816]{1,0:T(8,128)(2,1)} async-done(((bf16[512,2816]{1,0:T(8,128)(2,1)}), bf16[2048,2816]{1,0:T(8,128)(2,1)}) %all-gather.15.cloned.1.call-update) | async-done | bytes 11534352 | tf_op jit(solution)/shard_map/all_gather | solution.py:80
  267.7 9.0 fusion.109
  276.7 106.7 %all-gather.17.cloned.1.call-done = bf16[2048,2816]{1,0:T(8,128)(2,1)} async-done(((bf16[512,2816]{1,0:T(8,128)(2,1)}), bf16[2048,2816]{1,0:T(8,128)(2,1)}) %all-gather.17.cloned.1.call-update) | async-done | bytes 11534352 | tf_op jit(solution)/shard_map/all_gather | solution.py:81
  383.3 9.0 fusion.110
  392.3 106.5 %all-gather.19.cloned.1.call-done = bf16[2816,2048]{1,0:T(8,128)(2,1)} async-done(((bf16[2816,512]{1,0:T(8,128)(2,1)}), bf16[2816,2048]{1,0:T(8,128)(2,1)}) %all-gather.19.cloned.1.call-update) | async-done | bytes 11534352 | tf_op jit(solution)/shard_map/all_gather | solution.py:85
  498.8 11.4 multiply_convert_fusion
  517.4 8.5 fusion.68
  525.9 19.7 %all-reduce.13.cloned.1.call-done = bf16[256,2048]{1,0:T(8,128)(2,1)} async-done(((bf16[256,2048]{1,0:T(8,128)(2,1)}), bf16[256,2048]{1,0:T(8,128)(2,1)}) %all-reduce.13.cloned.1.call-update) | async-done | bytes 1048592 | tf_op jit(solution)/shard_map/psum | solution.py:175
  556.1 40.7 %while.41 = (s32[]{:T(128)}, f32[256,2,8,64]{0,3,2,1:T(8,128)S(1)}, bf16[2,512,2,64]{1,3,2,0:T(8,128)(2,1)}, bf16[2,512,2,64]{1,3,2,0:T(8,128)(2,1)}, bf16[2,512...) while((s32[]{:T(128)}, f32[256,2,8,64]{0,3,2,1:T(8,128)S(1)}, ...), condition=%wide.region_13.14_spmd.clone, body=%wide.region_12.13_spmd.clone.sunk | while | flops 1362034688 | bytes 96657208 | solution.py:215
  607.0 12.7 reduce-scatter.10.cloned.1.call-done
  622.2 18.5 %reduce-scatter.12.cloned.1.call-done = bf16[256,128]{0,1:T(8,128)(2,1)} async-done(((bf16[1024,128]{0,1:T(8,128)(2,1)}), bf16[256,128]{0,1:T(8,128)(2,1)}) %reduce-scatter.12.cloned.1.call-update) | async-done | bytes 65552 | tf_op jit(solution)/shard_map/reduce_scatter | solution.py:227
  671.8 9.1 convolution_convert_fusion.4
  684.8 10.4 reduce-scatter.20.cloned.1.call-done
  695.2 27.8 %reduce-scatter.16.cloned.1.call-done = bf16[512,128]{1,0:T(8,128)(2,1)} async-done(((bf16[2048,128]{1,0:T(8,128)(2,1)}), bf16[512,128]{1,0:T(8,128)(2,1)}) %reduce-scatter.16.cloned.1.call-update) | async-done | bytes 131088 | tf_op jit(solution)/shard_map/reduce_scatter | solution.py:265
  723.0 27.5 %reduce-scatter.18.cloned.1.call-done = bf16[512,128]{1,0:T(8,128)(2,1)} async-done(((bf16[2048,128]{1,0:T(8,128)(2,1)}), bf16[512,128]{1,0:T(8,128)(2,1)}) %reduce-scatter.18.cloned.1.call-update) | async-done | bytes 131088 | tf_op jit(solution)/shard_map/reduce_scatter | solution.py:268
  750.5 56.5 %reduce-scatter.14.cloned.1.call-done = bf16[512,1024]{1,0:T(8,128)(2,1)} async-done(((bf16[2048,1024]{1,0:T(8,128)(2,1)}), bf16[512,1024]{1,0:T(8,128)(2,1)}) %reduce-scatter.14.cloned.1.call-update) | async-done | bytes 1048592 | tf_op jit(solution)/shard_map/reduce_scatter | solution.py:262
  807.0 115.1 %reduce-scatter.22.cloned.1.call-done = bf16[512,2816]{1,0:T(8,128)(2,1)} async-done(((bf16[2048,2816]{1,0:T(8,128)(2,1)}), bf16[512,2816]{1,0:T(8,128)(2,1)}) %reduce-scatter.22.cloned.1.call-update) | async-done | bytes 2883600 | tf_op jit(solution)/shard_map/reduce_scatter | solution.py:277
  922.1 115.1 %reduce-scatter.24.cloned.1.call-done = bf16[512,2816]{1,0:T(8,128)(2,1)} async-done(((bf16[2048,2816]{1,0:T(8,128)(2,1)}), bf16[512,2816]{1,0:T(8,128)(2,1)}) %reduce-scatter.24.cloned.1.call-update) | async-done | bytes 2883600 | tf_op jit(solution)/shard_map/reduce_scatter | solution.py:280
  1037.2 115.1 %reduce-scatter.26.cloned.1.call-done = bf16[512,2816]{0,1:T(8,128)(2,1)} async-done(((bf16[2048,2816]{0,1:T(8,128)(2,1)}), bf16[512,2816]{0,1:T(8,128)(2,1)}) %reduce-scatter.26.cloned.1.call-update) | async-done | bytes 2883600 | tf_op jit(solution)/shard_map/reduce_scatter | solution.py:283
  1154.2 22.2 %all-reduce.17.cloned.1.call-done = (bf16[256,2048]{1,0:T(8,128)(2,1)}, bf16[256,2048]{1,0:T(8,128)(2,1)}) async-done(((bf16[256,2048]{1,0:T(8,128)(2,1)}, bf16[256,2048]{1,0:T(8,128)(2,1)}), (bf16[256,2048]{1,0:T(8,128)(2,1)}, bf16[256,2048]{1,0:T(8,128)(2,1)})) %all-reduce.17.cloned.1.call-update) | async-done | bytes 2097168 | tf_op jit(solution)/shard_map/psum | solution.py:160
  1178.5 10.3 all-reduce.4
  1188.9 12.2 all-reduce.2
  1207.5 52.6 %all-gather.21.cloned.1.call-done = bf16[2048,1024]{1,0:T(8,128)(2,1)} async-done(((bf16[512,1024]{1,0:T(8,128)(2,1)}), bf16[2048,1024]{1,0:T(8,128)(2,1)}) %all-gather.21.cloned.1.call-update) | async-done | bytes 4194320 | tf_op jit(solution)/shard_map/all_gather | solution.py:65
  1265.5 341.7 %all-reduce.15.cloned.1.call-done = (bf16[512,1024]{1,0:T(8,128)(2,1)}, bf16[512,128]{1,0:T(8,128)(2,1)}, bf16[512,128]{1,0:T(8,128)(2,1)}, bf16[512,2816]{1,0:T...) async-done(((bf16[512,1024]{1,0:T(8,128)(2,1)}, bf16[512,128]{1,0:T(8,128)(2,1)}, bf16[512,128]{1,0:T(8,128)(2,1)}, bf16[512,2816]{1,0:T(8,128)(2,1)}, ...) | async-done | bytes 9961488 | tf_op jit(solution)/shard_map/psum | solution.py:289
  (274 shorter events, 204.0 us)
Async XLA Ops:
  7.2 84.3 %all-gather.11.cloned.1.call-start = ((), (), s32[]{:S(2)}) async-start(), calls=%async_computation.9 | async-start | bytes 5242880 | tf_op jit(solution)/shard_map/all_gather | solution.py:76
  8.0 120.1 %all-gather.13.cloned.1.call-start = ((), (), s32[]{:S(2)}) async-start(), calls=%async_computation.10 | async-start | bytes 5242880 | tf_op jit(solution)/shard_map/all_gather | solution.py:84
  8.7 142.1 %all-reduce.11.cloned.1.call-start = ((), (), s32[]{:S(2)}) async-start(), calls=%async_computation.11 | async-start | bytes 2097152 | tf_op jit(solution)/shard_map/psum | solution.py:149
  18.4 79.6 %copy-start.32 = (f32[4,1,512]{2,1,0:T(1,128)}, f32[4,1,512]{2,1,0:T(1,128)S(1)}, u32[]{:S(2)}) copy-start(f32[4,1,512]{2,1,0:T(1,128)S(1)} %convert_element_type.288) | copy-start | bytes 24580
  18.7 79.3 %copy-start.43 = (f32[256]{0:T(256)}, f32[256]{0:T(256)S(1)}, u32[]{:S(2)}) copy-start(f32[256]{0:T(256)S(1)} %add_rsqrt_fusion.1) | copy-start | bytes 3076
  35.3 66.3 %copy-start.28 = (f32[256,32]{0,1:T(8,128)}, f32[256,32]{0,1:T(8,128)S(1)}, u32[]{:S(2)}) copy-start(f32[256,32]{0,1:T(8,128)S(1)} %get-tuple-element.449) | copy-start | bytes 98308
  35.3 17.7 %copy-start.34 = (s32[1,256]{1,0:T(1,128)S(1)}, s32[1,256]{1,0:T(1,128)}, u32[]{:S(2)}) copy-start(s32[1,256]{1,0:T(1,128)} %param.21) | copy-start | bytes 3076
  132.7 134.9 %all-gather.15.cloned.1.call-start = ((), (), s32[]{:S(2)}) async-start(), calls=%async_computation.12 | async-start | bytes 14417920 | tf_op jit(solution)/shard_map/all_gather | solution.py:80
  133.3 250.0 %all-gather.17.cloned.1.call-start = ((), (), s32[]{:S(2)}) async-start(), calls=%async_computation.13 | async-start | bytes 14417920 | tf_op jit(solution)/shard_map/all_gather | solution.py:81
  133.9 364.9 %all-gather.19.cloned.1.call-start = ((), (), s32[]{:S(2)}) async-start(), calls=%async_computation.14 | async-start | bytes 14417920 | tf_op jit(solution)/shard_map/all_gather | solution.py:85
  134.5 411.1 %all-reduce.13.cloned.1.call-start = ((), (), s32[]{:S(2)}) async-start(), calls=%async_computation.15 | async-start | bytes 2097152 | tf_op jit(solution)/shard_map/psum | solution.py:175
  152.5 448.4 %copy-start.46 = (f32[256]{0:T(256)}, f32[256]{0:T(256)S(1)}, u32[]{:S(2)}) copy-start(f32[256]{0:T(256)S(1)} %add_rsqrt_fusion) | copy-start | bytes 3076
  153.1 230.3 %copy-start.6 = (bf16[256,2048]{1,0:T(8,128)(2,1)}, bf16[256,2048]{1,0:T(8,128)(2,1)S(1)}, u32[]{:S(2)}) copy-start(bf16[256,2048]{1,0:T(8,128)(2,1)S(1)} %multiply_convert_fusion.3) | copy-start | bytes 3145732
  525.8 93.9 %reduce-scatter.10.cloned.1.call-start = ((), (), s32[]{:S(2)}) async-start(), calls=%async_computation.16 | async-start | bytes 327680 | tf_op jit(solution)/shard_map/reduce_scatter | solution.py:221
  548.8 52.1 %copy-start.49 = (f32[256]{0:T(256)}, f32[256]{0:T(256)S(1)}, u32[]{:S(2)}) copy-start(f32[256]{0:T(256)S(1)} %broadcast_multiply_fusion.1) | copy-start | bytes 3076
  598.8 41.9 %reduce-scatter.12.cloned.1.call-start = ((), (), s32[]{:S(2)}) async-start(), calls=%async_computation.17 | async-start | bytes 327680 | tf_op jit(solution)/shard_map/reduce_scatter | solution.py:227
  600.9 94.3 %reduce-scatter.20.cloned.1.call-start = ((), (), s32[]{:S(2)}) async-start(), calls=%async_computation.21 | async-start | bytes 5242880 | tf_op jit(solution)/shard_map/reduce_scatter | solution.py:271
  607.0 116.0 %reduce-scatter.16.cloned.1.call-start = ((), (), s32[]{:S(2)}) async-start(), calls=%async_computation.19 | async-start | bytes 655360 | tf_op jit(solution)/shard_map/reduce_scatter | solution.py:265
  620.7 22.3 %copy-start.35 = (bf16[256,2,64]{0,2,1:T(8,128)(2,1)}, bf16[256,2,64]{0,2,1:T(8,128)(2,1)S(1)}, u32[]{:S(2)}) copy-start(bf16[256,2,64]{0,2,1:T(8,128)(2,1)S(1)} %maximum_convert_fusion.1) | copy-start | bytes 196612
  622.1 128.3 %reduce-scatter.18.cloned.1.call-start = ((), (), s32[]{:S(2)}) async-start(), calls=%async_computation.20 | async-start | bytes 655360 | tf_op jit(solution)/shard_map/reduce_scatter | solution.py:268
  643.0 164.0 %reduce-scatter.14.cloned.1.call-start = ((), (), s32[]{:S(2)}) async-start(), calls=%async_computation.18 | async-start | bytes 5242880 | tf_op jit(solution)/shard_map/reduce_scatter | solution.py:262
  647.5 274.6 %reduce-scatter.22.cloned.1.call-start = ((), (), s32[]{:S(2)}) async-start(), calls=%async_computation.22 | async-start | bytes 14417920 | tf_op jit(solution)/shard_map/reduce_scatter | solution.py:277
  655.6 381.6 %reduce-scatter.24.cloned.1.call-start = ((), (), s32[]{:S(2)}) async-start(), calls=%async_computation.23 | async-start | bytes 14417920 | tf_op jit(solution)/shard_map/reduce_scatter | solution.py:280
  663.1 489.3 %reduce-scatter.26.cloned.1.call-start = ((), (), s32[]{:S(2)}) async-start(), calls=%async_computation.24 | async-start | bytes 14417920 | tf_op jit(solution)/shard_map/reduce_scatter | solution.py:283
  671.7 504.7 %all-reduce.17.cloned.1.call-start = ((), (), s32[]{:S(2)}) async-start(), calls=%async_computation.27 | async-start | bytes 4194304 | tf_op jit(solution)/shard_map/psum | solution.py:160
  684.7 575.4 %all-gather.21.cloned.1.call-start = ((), (), s32[]{:S(2)}) async-start(), calls=%async_computation.25 | async-start | bytes 5242880 | tf_op jit(solution)/shard_map/all_gather | solution.py:65
  695.2 912.0 %all-reduce.15.cloned.1.call-start = ((), (), s32[]{:S(2)}) async-start(), calls=%async_computation.26 | async-start | bytes 19922944 | tf_op jit(solution)/shard_map/psum | solution.py:289
  1152.3 24.1 %copy-start.45 = (f32[256]{0:T(256)S(1)}, f32[256]{0:T(256)}, u32[]{:S(2)}) copy-start(f32[256]{0:T(256)} %copy-done.43) | copy-start | bytes 3076
  1152.3 26.1 %copy-start.48 = (bf16[2048]{0:T(1024)(128)(2,1)S(1)}, bf16[2048]{0:T(1024)(128)(2,1)}, u32[]{:S(2)}) copy-start(bf16[2048]{0:T(1024)(128)(2,1)} %get-tuple-element.358) | copy-start | bytes 12292
  1152.4 50.0 %copy-start.5 = (bf16[256,2048]{1,0:T(8,128)(2,1)S(1)}, bf16[256,2048]{1,0:T(8,128)(2,1)}, u32[]{:S(2)}) copy-start(bf16[256,2048]{1,0:T(8,128)(2,1)} %all-reduce.11.cloned.1.call-done) | copy-start | bytes 3145732
  1152.4 50.0 %copy-start.47 = (f32[256]{0:T(256)S(1)}, f32[256]{0:T(256)}, u32[]{:S(2)}) copy-start(f32[256]{0:T(256)} %copy-done.46) | copy-start | bytes 3076
  1152.4 49.9 %copy-start.50 = (f32[256]{0:T(256)S(1)}, f32[256]{0:T(256)}, u32[]{:S(2)}) copy-start(f32[256]{0:T(256)} %copy-done.49) | copy-start | bytes 3076
  (47 other events, 229.3 us)
Sparse Core Ops, SparseCore 0:
  9.9 61.2 all-gather.10
  73.1 53.3 all-gather.12
  132.8 17.9 all-reduce.10
  152.6 114.9 all-gather.14
  269.5 113.7 all-gather.16
  385.1 113.6 all-gather.18
  526.0 19.5 all-reduce.12
  599.0 20.7 reduce-scatter.9
  622.7 17.9 reduce-scatter.11
  644.1 51.0 reduce-scatter.19
  698.2 24.7 reduce-scatter.15
  725.7 24.7 reduce-scatter.17
  754.3 52.6 reduce-scatter.13
  810.0 112.1 reduce-scatter.21
  925.1 112.0 reduce-scatter.23
  1040.2 112.0 reduce-scatter.25
  1155.1 21.2 all-reduce.16
  1177.9 82.1 all-gather.20
  1263.7 343.4 all-reduce.14
